TPU v7x, 32 devices: a whole 2x2x4 slice. The times are simulated.
32 devices in a mesh: grp: 2 (over x), ord: 16 (over z, y, core).
Axes of the slice: x: 2, y: 2, z: 4, core: 2. Of those that a mesh axis runs over, the one named last changes fastest.
Arguments:
- grid: bfloat16 [1024, 1024, 256], P(('grp', 'ord')), parts along dimension 0, may hold values from -6 to 6
- legendre: bfloat16 [16, 64, 512, 512], P('ord'), as said below
- mixing: bfloat16 [512, 2, 256, 256], P('ord'), may hold values from -0.25 to 0.25
Outputs:
- spectrum: bfloat16 [1024, 512, 512], P(('grp', 'ord')), parts along dimension 0
There are 2 independent parts, one for each index of `grp`. A program takes and returns all parts, laid end to end along the dimension named above; an argument that names none is the same for every part. Nothing has to cross between parts.
Inputs may be any that keep to these rules, and one draw needn't show every extreme that they name: `legendre`: entries whose degree is below their order are zero. The slots 32 to 63 of block index b repeat the panels that block index 16 - 1 - b holds in its slots 0 to 31.
All inputs are finite; a program needn't handle non-finite values.
Results may differ from a plain program's by a relative error of at most 0.0062.
Values may be sent and summed in bfloat16 or wider, within the bound.
No kernel may reach another device: no remote copies, remote signals or barrier semaphores. Data moves between devices by JAX's collectives and lax.ppermute only.
A program may use at most 256 MiB of HBM per device.

v0:
```python
import math
import jax
import jax.numpy as jnp
from jax import lax
from jax.sharding import PartitionSpec as P

DEG_TILE = 128


def fourier_table(nlon, orders):
    longitude = jnp.arange(nlon, dtype=jnp.int32)
    order = jnp.arange(orders, dtype=jnp.int32)
    phase = longitude[:, None] * order[None, :] % nlon
    angle = phase.astype(jnp.float32) * (2.0 * math.pi / nlon)
    scale = 1.0 / math.sqrt(nlon)
    table = jnp.stack([jnp.cos(angle) * scale, -jnp.sin(angle) * scale], axis=-1)
    return table.reshape(nlon, 2 * orders).astype(jnp.bfloat16)


def legendre_tiles(panel, arrived, first):
    groups, degrees, latitudes = panel.shape
    width = arrived.shape[2]
    buffer = jnp.zeros((groups, degrees, width), jnp.float32)

    def advance(index, current):
        start = index * DEG_TILE
        piece = lax.dynamic_slice_in_dim(panel, start, DEG_TILE, 1)
        part = jnp.einsum("mlt,tmk->mlk", piece, arrived, preferred_element_type=jnp.float32)
        return lax.dynamic_update_slice_in_dim(current, part, start, 1)

    return lax.fori_loop(first, degrees // DEG_TILE, advance, buffer).astype(jnp.bfloat16)


def on_device(grid, legendre, mixing):
    count = lax.axis_size("ord")
    block = lax.axis_index("ord")
    lat_rows, nlon, chans = grid.shape
    panels = legendre[0]
    per_dev = panels.shape[0] // 2
    orders = per_dev * count
    table = fourier_table(nlon, orders)
    spectra = jnp.einsum("tnc,nk->tkc", grid, table, preferred_element_type=jnp.float32).astype(
        jnp.bfloat16
    )
    sending = spectra.reshape(lat_rows, orders, 2 * chans)
    arrived = lax.all_to_all(sending, "ord", split_axis=1, concat_axis=0, tiled=True)
    first = per_dev * block // DEG_TILE
    coeffs = legendre_tiles(panels[:per_dev], arrived, first)
    landed = lax.all_to_all(coeffs, "ord", split_axis=1, concat_axis=0, tiled=True)
    real_part = mixing[:, 0]
    imag_part = mixing[:, 1]
    block_weight = jnp.concatenate(
        [
            jnp.concatenate([real_part, imag_part], axis=-1),
            jnp.concatenate([-imag_part, real_part], axis=-1),
        ],
        axis=1,
    )
    mixed = jnp.einsum("mlk,lkn->lmn", landed, block_weight, preferred_element_type=jnp.float32)
    return mixed.astype(jnp.bfloat16)


def solution(mesh):
    return jax.shard_map(
        on_device,
        mesh=mesh,
        in_specs=(
            P(("grp", "ord"), None, None),
            P("ord", None, None, None),
            P("ord", None, None, None),
        ),
        out_specs=P(("grp", "ord"), None, None),
        check_vma=False,
    )
```

profile of v0, /device:TPU:18, one launch (start us, length us, event | category | flops | bytes accessed | tf_op | source)
XLA Modules:
  0.0 919.4 jit_solution(554978800378174407)
XLA Ops:
  0.0 8.6 multiply_convert_fusion
  8.6 0.2 pad_maximum_fusion
  8.8 3.9 copy.20
  12.8 2.7 reshape.84
  15.5 25.9 %convert_bitcast_fusion = bf16[32,1024,256]{2,1,0:T(8,128)(2,1)} fusion(bf16[1024,1024,1]{0,1,2:T(8,128)(2,1)S(1)} %reshape.84, bf16[32,1024,256]{2,1,0:T(8,128)(2,1)} %param.5), kind=kOutput, calls=%fused_computation.12 | convolution fusion | flops 17188257792 | bytes 35651584 | tf_op jit(solution)/shard_map/tnc,nk->tkc/dot_general | solution.py:42
  41.4 24.5 %reshape.83 = bf16[32,512,512]{2,1,0:T(8,128)(2,1)} reshape(bf16[32,1024,256]{2,1,0:T(8,128)(2,1)} %convert_bitcast_fusion) | data formatting | bytes 33554432 | tf_op jit(solution)/shard_map/reshape | solution.py:45
  65.9 18.5 %copy.21 = bf16[32,512,512]{2,0,1:T(8,128)(2,1)} copy(bf16[32,512,512]{2,1,0:T(8,128)(2,1)} %reshape.83) | data formatting | bytes 33554432 | tf_op jit(solution)/shard_map/reshape | solution.py:45
  84.3 6.2 all-to-all-start
  90.5 13.7 %slice_bitcast_fusion = bf16[32,512,512]{2,1,0:T(8,128)(2,1)} fusion(bf16[1,64,512,512]{3,2,1,0:T(8,128)(2,1)} %param.6), kind=kLoop, calls=%fused_computation.13 | loop fusion | bytes 33554432 | tf_op jit(solution)/shard_map/slice | solution.py:48
  104.2 348.6 %all-to-all-done = bf16[32,512,512]{2,0,1:T(8,128)(2,1)} async-done(((bf16[32,512,512]{2,0,1:T(8,128)(2,1)}), bf16[32,512,512]{2,0,1:T(8,128)(2,1)}, u32[]{:S(2)}, u32[]{:S(2)}) %all-to-all-start) | async-done | bytes 16777248 | tf_op jit(solution)/shard_map/all_to_all | solution.py:46
  452.9 14.1 %copy.22 = bf16[16,32,32,512]{3,1,0,2:T(8,128)(2,1)} copy(bf16[16,32,32,512]{3,1,2,0:T(8,128)(2,1)} %bitcast.3) | data formatting | bytes 33554432 | tf_op jit(solution)/shard_map/all_to_all | solution.py:46
  466.9 6.1 broadcast_in_dim.2.clone
  473.1 27.6 %while.10 = (s32[]{:T(128)}, bf16[32,512,512]{2,0,1:T(8,128)(2,1)}, bf16[32,512,512]{2,1,0:T(8,128)(2,1)}, bf16[512,32,512]{2,0,1:T(8,128)(2,1)}, s32[]{:T(128)}, /*index=5*/s32[]{:T(128)}, s32[]{:T(128)}, s32[]{:T(128)}) while((s32[]{:T(128)}, bf16[32,512,512]{2,0,1:T(8,128)(2,1)}, bf16[32,512,512]{2,1,0:T(8,128)(2,1)}, ...), condition=%wide.region_1.2_spmd, body=%wide.region_0.1_spmd.sunk | while | flops 2147483648 | bytes 33554568 | solution.py:31
  473.1 9.4 %fusion.31 = bf16[32,128,512]{2,1,0:T(8,128)(2,1)S(1)} fusion(bf16[512,32,512]{2,0,1:T(8,128)(2,1)} %get-tuple-element.84, bf16[32,512,512]{2,1,0:T(8,128)(2,1)} %get-tuple-element.83, s32[]{:T(128)S(6)} %select_n.40), kind=kOutput, calls=%fused_computation.1.clone.1 | convolution fusion | flops 2147483648 | bytes 25165828 | tf_op jit(solution)/shard_map/while/body/mlt,tmk->mlk/dot_general | solution.py:28
  482.5 4.4 copy_dynamic-update-slice_fusion.2
  486.9 9.4 %fusion.31 = bf16[32,128,512]{2,1,0:T(8,128)(2,1)S(1)} fusion(bf16[512,32,512]{2,0,1:T(8,128)(2,1)} %get-tuple-element.84, bf16[32,512,512]{2,1,0:T(8,128)(2,1)} %get-tuple-element.83, s32[]{:T(128)S(6)} %select_n.40), kind=kOutput, calls=%fused_computation.1.clone.1 | convolution fusion | flops 2147483648 | bytes 25165828 | tf_op jit(solution)/shard_map/while/body/mlt,tmk->mlk/dot_general | solution.py:28
  496.3 4.4 copy_dynamic-update-slice_fusion.2
  500.6 17.6 %all-to-all-start.1 = ((bf16[32,512,512]{2,0,1:T(8,128)(2,1)}), bf16[32,512,512]{2,0,1:T(8,128)(2,1)}, u32[]{:S(2)}, u32[]{:S(2)}) async-start(bf16[32,512,512]{2,0,1:T(8,128)(2,1)} %get-tuple-element.27), calls=%async_computation.1 | async-start | bytes 33554432 | tf_op jit(solution)/shard_map/all_to_all | solution.py:49
  518.3 4.4 fusion.21
  522.7 5.9 slice_bitcast_fusion.1
  528.5 352.9 %all-to-all-done.1 = bf16[32,512,512]{2,0,1:T(8,128)(2,1)} async-done(((bf16[32,512,512]{2,0,1:T(8,128)(2,1)}), bf16[32,512,512]{2,0,1:T(8,128)(2,1)}, u32[]{:S(2)}, u32[]{:S(2)}) %all-to-all-start.1) | async-done | bytes 16777248 | tf_op jit(solution)/shard_map/all_to_all | solution.py:49
  881.4 0.0 copy-start
  881.4 14.4 %copy.24 = bf16[32,16,32,512]{3,0,1,2:T(8,128)(2,1)} copy(bf16[32,16,32,512]{3,0,2,1:T(8,128)(2,1)} %bitcast.5) | data formatting | bytes 33554432 | tf_op jit(solution)/shard_map/all_to_all | solution.py:49
  895.8 0.0 copy-done
  895.8 23.6 %fusion.11 = bf16[32,512,512]{2,1,0:T(8,128)(2,1)} fusion(bf16[512,32,512]{2,0,1:T(8,128)(2,1)} %bitcast.31, bf16[32,256,256]{2,1,0:T(8,128)(2,1)} %get-tuple-element.37, bf16[32,256,256]{2,1,0:T(8,128)(2,1)S(1)} %copy-done, bf16[32,256,256]{2,1,0:T(8,128)(2,1)} %get-tuple-element.36), kind=kOutput, calls=%fused_computation.14 | convolution fusion | flops 8665432064 | bytes 46137344 | tf_op jit(solution)/shard_map/mlk,lkn->lmn/dot_general | solution.py:59
Async XLA Ops:
  84.3 368.5 %all-to-all-start = ((bf16[32,512,512]{2,0,1:T(8,128)(2,1)}), bf16[32,512,512]{2,0,1:T(8,128)(2,1)}, u32[]{:S(2)}, u32[]{:S(2)}) async-start(bf16[32,512,512]{2,0,1:T(8,128)(2,1)} %copy.21), calls=%async_computation | async-start | bytes 33554432 | tf_op jit(solution)/shard_map/all_to_all | solution.py:46
  500.6 380.8 %all-to-all-start.1 = ((bf16[32,512,512]{2,0,1:T(8,128)(2,1)}), bf16[32,512,512]{2,0,1:T(8,128)(2,1)}, u32[]{:S(2)}, u32[]{:S(2)}) async-start(bf16[32,512,512]{2,0,1:T(8,128)(2,1)} %get-tuple-element.27), calls=%async_computation.1 | async-start | bytes 33554432 | tf_op jit(solution)/shard_map/all_to_all | solution.py:49
  881.4 14.4 %copy-start = (bf16[32,256,256]{2,1,0:T(8,128)(2,1)S(1)}, bf16[32,256,256]{2,1,0:T(8,128)(2,1)}, u32[]{:S(2)}) copy-start(bf16[32,256,256]{2,1,0:T(8,128)(2,1)} %fusion.21) | copy-start | bytes 12582916
where the time goes:
time: 921 us; the launch traced here: 919 us
  waiting for transfers between devices  701 us (76%)
  local copies, waits for them, and re-layouts  113 us (12%)
  matrix products  68.3 us (7%)
  starting transfers between devices  23.8 us (3%)
  other arithmetic  13.2 us (1%)
    all_to_all x1, waiting for transfers between devices, on_device(): lax.all_to_all(coeffs, 'ord', split_axis=1, concat_axis=0, tiled=True)  353 us
    all_to_all x1, waiting for transfers between devices, on_device(): lax.all_to_all(sending, 'ord', split_axis=1, concat_axis=0, tiled=True)  349 us
    reshape x2, local copies, waits for them, and re-layouts, on_device(): sending = spectra.reshape(lat_rows, orders, 2 * chans)  43 us
    dot_general x1, matrix products, on_device(): jnp.einsum('tnc,nk->tkc', grid, table, preferred_element_type=jnp.float32)  25.9 us
    dot_general x1, matrix products, on_device(): jnp.einsum('mlk,lkn->lmn', landed, block_weight, preferred_element_type=j...  23.6 us
    dot_general x2, matrix products, advance(): jnp.einsum('mlt,tmk->mlk', piece, arrived, preferred_element_type=jnp.flo...  18.8 us
  transfers between devices with their start and end apart: 2, of which 2 were waited for; matrix products, arithmetic and copies ran while one was open for 3% of the time, Pallas kernels for 0%

commit v1 on v0

--- a/solution.py
+++ b/solution.py
@@ -5,6 +5,12 @@
 from jax.sharding import PartitionSpec as P
 
 DEG_TILE = 128
+
+
+def exchange_blocks(x, mesh_axis, split, join):
+    pieces = jnp.split(x, lax.axis_size(mesh_axis), axis=split)
+    received = lax.all_to_all(jnp.stack(pieces), mesh_axis, 0, 0)
+    return jnp.concatenate(received, axis=join)
 
 
 def fourier_table(nlon, orders):
@@ -43,7 +49,7 @@
         jnp.bfloat16
     )
     sending = spectra.reshape(lat_rows, orders, 2 * chans)
-    arrived = lax.all_to_all(sending, "ord", split_axis=1, concat_axis=0, tiled=True)
+    arrived = exchange_blocks(sending, "ord", 1, 0)
     first = per_dev * block // DEG_TILE
     coeffs = legendre_tiles(panels[:per_dev], arrived, first)
     landed = lax.all_to_all(coeffs, "ord", split_axis=1, concat_axis=0, tiled=True)

time: 921 us -> 942 us (1.023)
  local copies, waits for them, and re-layouts: 113 us -> 134 us
    unnamed x2 -> x17, local copies, waits for them, and re-layouts: 0.01 us -> 34.6 us
    reshape x2 -> x1, local copies, waits for them, and re-layouts: 43 us -> 24.5 us  [on_device(): sending = spectra.reshape(lat_rows, orders, 2 * chans)]
where the time goes in v1:
time: 942 us; the launch traced here: 941 us
  waiting for transfers between devices  701 us (74%)
  local copies, waits for them, and re-layouts  134 us (14%)
  matrix products  68.3 us (7%)
  starting transfers between devices  23.8 us (3%)
  other arithmetic  13.2 us (1%)
    all_to_all x1, waiting for transfers between devices, on_device(): lax.all_to_all(coeffs, 'ord', split_axis=1, concat_axis=0, tiled=True)  353 us
    all_to_all x1, waiting for transfers between devices, exchange_blocks(): received = lax.all_to_all(jnp.stack(pieces), mesh_axis, 0, 0)  349 us
    unnamed x17, local copies, waits for them, and re-layouts  34.6 us
    dot_general x1, matrix products, on_device(): jnp.einsum('tnc,nk->tkc', grid, table, preferred_element_type=jnp.float32)  25.9 us
    reshape x1, local copies, waits for them, and re-layouts, on_device(): sending = spectra.reshape(lat_rows, orders, 2 * chans)  24.5 us
    dot_general x1, matrix products, on_device(): jnp.einsum('mlk,lkn->lmn', landed, block_weight, preferred_element_type=j...  23.6 us
  transfers between devices with their start and end apart: 2, of which 2 were waited for; matrix products, arithmetic and copies ran while one was open for 3% of the time, Pallas kernels for 0%

profile of v1, /device:TPU:18, one launch (start us, length us, event | category | flops | bytes accessed | tf_op | source)
XLA Modules:
  0.0 940.6 jit_solution(12287359795954431029)
XLA Ops:
  0.0 8.6 multiply_convert_fusion
  8.6 0.2 pad_maximum_fusion
  8.8 3.9 copy.18
  12.8 2.7 reshape.88
  15.5 25.9 %convert_bitcast_fusion = bf16[32,1024,256]{2,1,0:T(8,128)(2,1)} fusion(bf16[1024,1024,1]{0,1,2:T(8,128)(2,1)S(1)} %reshape.88, bf16[32,1024,256]{2,1,0:T(8,128)(2,1)} %param.5), kind=kOutput, calls=%fused_computation.12 | convolution fusion | flops 17188257792 | bytes 35651584 | tf_op jit(solution)/shard_map/tnc,nk->tkc/dot_general | solution.py:48
  41.4 24.5 %reshape.86 = bf16[32,512,512]{2,1,0:T(8,128)(2,1)} reshape(bf16[32,1024,256]{2,1,0:T(8,128)(2,1)} %convert_bitcast_fusion) | data formatting | bytes 33554432 | tf_op jit(solution)/shard_map/reshape | solution.py:51
  65.9 2.3 fusion.35
  68.2 2.3 fusion.34
  70.5 2.3 fusion.33
  72.8 2.3 fusion.32
  75.1 2.3 fusion.31
  77.4 2.3 fusion.30
  79.7 2.3 fusion.29
  82.0 2.3 fusion.28
  84.3 2.3 fusion.27
  86.6 2.3 fusion.26
  89.0 2.3 fusion.25
  91.3 2.3 fusion.24
  93.6 2.3 fusion.23
  95.9 2.3 fusion.22
  98.2 2.3 fusion.21
  100.5 2.3 fusion.20
  102.8 6.2 all-to-all-start
  109.0 13.7 %slice_bitcast_fusion = bf16[32,512,512]{2,1,0:T(8,128)(2,1)} fusion(bf16[1,64,512,512]{3,2,1,0:T(8,128)(2,1)} %param.6), kind=kLoop, calls=%fused_computation.13 | loop fusion | bytes 33554432 | tf_op jit(solution)/shard_map/slice | solution.py:54
  122.7 348.6 %all-to-all-done = bf16[16,32,32,512]{3,2,1,0:T(8,128)(2,1)} async-done(((bf16[16,32,32,512]{3,2,1,0:T(8,128)(2,1)}), bf16[16,32,32,512]{3,2,1,0:T(8,128)(2,1)}, u32[]{:S(2)}, u32[]{:S(2)}) %all-to-all-start) | async-done | bytes 16777248 | tf_op jit(solution)/shard_map/all_to_all | solution.py:12
  471.3 16.8 %copy.19 = bf16[16,32,32,512]{3,1,0,2:T(8,128)(2,1)} copy(bf16[16,32,32,512]{3,2,1,0:T(8,128)(2,1)} %all-to-all-done) | data formatting | bytes 33554432 | tf_op jit(solution)/shard_map/all_to_all | solution.py:12
  488.1 6.1 broadcast_in_dim.2.clone
  494.2 27.6 %while.10 = (s32[]{:T(128)}, bf16[32,512,512]{2,0,1:T(8,128)(2,1)}, bf16[32,512,512]{2,1,0:T(8,128)(2,1)}, bf16[512,32,512]{2,0,1:T(8,128)(2,1)}, s32[]{:T(128)}, /*index=5*/s32[]{:T(128)}, s32[]{:T(128)}, s32[]{:T(128)}) while((s32[]{:T(128)}, bf16[32,512,512]{2,0,1:T(8,128)(2,1)}, bf16[32,512,512]{2,1,0:T(8,128)(2,1)}, ...), condition=%wide.region_1.2_spmd, body=%wide.region_0.1_spmd.sunk | while | flops 2147483648 | bytes 33554568 | solution.py:37
  494.2 9.4 fusion.47
  503.6 4.4 copy_dynamic-update-slice_fusion.2
  508.0 9.4 fusion.47
  517.4 4.4 copy_dynamic-update-slice_fusion.2
  521.8 17.6 %all-to-all-start.1 = ((bf16[32,512,512]{2,0,1:T(8,128)(2,1)}), bf16[32,512,512]{2,0,1:T(8,128)(2,1)}, u32[]{:S(2)}, u32[]{:S(2)}) async-start(bf16[32,512,512]{2,0,1:T(8,128)(2,1)} %get-tuple-element.27), calls=%async_computation.1 | async-start | bytes 33554432 | tf_op jit(solution)/shard_map/all_to_all | solution.py:55
  539.4 4.4 fusion.37
  543.8 5.9 slice_bitcast_fusion.1
  549.7 352.9 %all-to-all-done.1 = bf16[32,512,512]{2,0,1:T(8,128)(2,1)} async-done(((bf16[32,512,512]{2,0,1:T(8,128)(2,1)}), bf16[32,512,512]{2,0,1:T(8,128)(2,1)}, u32[]{:S(2)}, u32[]{:S(2)}) %all-to-all-start.1) | async-done | bytes 16777248 | tf_op jit(solution)/shard_map/all_to_all | solution.py:55
  902.5 0.0 copy-start
  902.6 14.4 %copy.21 = bf16[32,16,32,512]{3,0,1,2:T(8,128)(2,1)} copy(bf16[32,16,32,512]{3,0,2,1:T(8,128)(2,1)} %bitcast.19) | data formatting | bytes 33554432 | tf_op jit(solution)/shard_map/all_to_all | solution.py:55
  916.9 0.0 copy-done
  916.9 23.6 %fusion.11 = bf16[32,512,512]{2,1,0:T(8,128)(2,1)} fusion(bf16[512,32,512]{2,0,1:T(8,128)(2,1)} %bitcast.92, bf16[32,256,256]{2,1,0:T(8,128)(2,1)} %get-tuple-element.37, bf16[32,256,256]{2,1,0:T(8,128)(2,1)S(1)} %copy-done, bf16[32,256,256]{2,1,0:T(8,128)(2,1)} %get-tuple-element.36), kind=kOutput, calls=%fused_computation.14 | convolution fusion | flops 8665432064 | bytes 46137344 | tf_op jit(solution)/shard_map/mlk,lkn->lmn/dot_general | solution.py:65
Async XLA Ops:
  102.8 368.5 %all-to-all-start = ((bf16[16,32,32,512]{3,2,1,0:T(8,128)(2,1)}), bf16[16,32,32,512]{3,2,1,0:T(8,128)(2,1)}, u32[]{:S(2)}, u32[]{:S(2)}) async-start(bf16[16,32,32,512]{3,2,1,0:T(8,128)(2,1)} %fusion.20), calls=%async_computation | async-start | bytes 33554432 | tf_op jit(solution)/shard_map/all_to_all | solution.py:12
  521.8 380.8 %all-to-all-start.1 = ((bf16[32,512,512]{2,0,1:T(8,128)(2,1)}), bf16[32,512,512]{2,0,1:T(8,128)(2,1)}, u32[]{:S(2)}, u32[]{:S(2)}) async-start(bf16[32,512,512]{2,0,1:T(8,128)(2,1)} %get-tuple-element.27), calls=%async_computation.1 | async-start | bytes 33554432 | tf_op jit(solution)/shard_map/all_to_all | solution.py:55
  902.5 14.4 %copy-start = (bf16[32,256,256]{2,1,0:T(8,128)(2,1)S(1)}, bf16[32,256,256]{2,1,0:T(8,128)(2,1)}, u32[]{:S(2)}) copy-start(bf16[32,256,256]{2,1,0:T(8,128)(2,1)} %fusion.37) | copy-start | bytes 12582916
